TPU v7x, 32 devices: a whole 2x2x4 slice. The times are simulated.
32 devices in a mesh: lat: 4 (over z), lon: 8 (over y, x, core).
Axes of the slice: x: 2, y: 2, z: 4, core: 2. Of those that a mesh axis runs over, the one named last changes fastest.
Arguments:
- winds: bfloat16 [16, 32, 3, 40, 128], P('lat', 'lon'), may hold values from -6 to 6
- positions: float32 [4096, 3, 128], P(('lat', 'lon')), may hold values from 0 to 39, as said below
- velocity: float32 [4096, 3, 128], P(('lat', 'lon')), may hold values from -6 to 6
- increments: float32 [4096, 3, 128], P(('lat', 'lon')), may hold values from -6 to 6
- mass: float32 [4096, 8, 128], P(('lat', 'lon')), may hold values from 0.1 to 1
- requests: int32 [32, 32, 2], P(('lat', 'lon')), may hold values from 0 to 15
- block_slots: int32 [4096, 1], P(('lat', 'lon')), may hold values from 0 to 63; in each aligned block of 128 rows (0 to 127, 128 to 255, ...) at most 8 rows name the same one
- destinations: int32 [4096, 1], P(('lat', 'lon')), may hold values from 0 to 31; in each aligned block of 128 rows (0 to 127, 128 to 255, ...) at most 8 rows name the same one
- cell_keys: int32 [4096, 128], P(('lat', 'lon')), may hold values from 0 to 2047, as said below
Outputs:
- moved: float32 [4096, 3, 128], P(('lat', 'lon'))
- turbulence: float32 [4096, 3, 128], P(('lat', 'lon'))
- concentration: float32 [16, 32, 8, 40, 128], P('lat', 'lon')
Inputs may be any that keep to these rules, and one draw needn't show every extreme that they name: `positions`: component 0 (cell row) lies in 0 to 7, component 1 (cell column) in 0 to 15, component 2 (level) in 0 to 39. requests[o, t, k] names a met block of tile t by its local number. `block_slots`: slot k stands for the (k % 2)-th request that the owner sends to tile k // 2; of the 128 blocks of one owner at most 8 have the same slot, and on some owners one slot gets exactly 8. `destinations`: of the 128 blocks of one owner at most 8 have the same destination; on some owners one destination gets exactly 8. `cell_keys`: a key is (local met block) * 128 + cell of the destination tile; all keys of one particle block lie in one met block.
All inputs are finite; a program needn't handle non-finite values.
Results may differ from a plain program's by a relative error of at most 0.0027.
Values may be sent and summed in bfloat16 or wider, within the bound.
A program may use at most 64 MiB of HBM per device.

v0:
```python
import functools

import jax
import jax.numpy as jnp
from jax import lax
from jax.experimental import pallas as pl
from jax.experimental.pallas import tpu as pltpu
from jax.sharding import PartitionSpec as P

BY = 8
BX = 16
MBC = 128
LEV = 40
S = 8
BLK = 128
MBR = 4
MBK = 4
Q = 2
MB = MBR * MBK

DECAY = 0.8
KICK = 0.6
STEP = 0.5

FULL = 65535.0
GUST = 6.1
BUNCH = 4
SHIFT = 64
CHUNKS = 4
SPLIT = 16
SPAN = LEV - SPLIT
VMEM = pl.BlockSpec(memory_space=pltpu.VMEM)
SMEM = pl.BlockSpec(memory_space=pltpu.SMEM)


def up8(rows):
    return -(-rows // 8) * 8


def hat(offset):
    return jnp.maximum(0.0, 1.0 - jnp.abs(offset))


def low(word):
    return (word & 0xFFFF).astype(jnp.float32)


def high(word):
    return lax.shift_right_logical(word, 16).astype(jnp.float32)


def code(value, scale):
    return (value * scale + 0.5).astype(jnp.int32)


def aligned(start):
    return pl.multiple_of(start, 8)


def bits(mask):
    return jnp.where(mask, 1.0, 0.0).astype(jnp.bfloat16)


def halves(value):
    top = (value >> 8).astype(jnp.float32).astype(jnp.bfloat16)
    return top, (value & 255).astype(jnp.float32).astype(jnp.bfloat16)


def product(left, right):
    return jnp.dot(left, right, preferred_element_type=jnp.float32)


def chooser(place, pairs):
    index = lax.broadcasted_iota(jnp.int32, (pairs, place.shape[1]), 0)
    picks = jnp.concatenate(
        [jnp.where(place == 2 * index + odd, 1.0, 0.0) for odd in range(2)], axis=0
    )
    return jnp.concatenate([picks * 256.0, picks], axis=1).astype(jnp.bfloat16)


def chosen(picks, values):
    pairs = picks.shape[0] // 2
    parts = [halves(value) for value in values]
    data = jnp.concatenate(
        [
            jnp.concatenate([top for top, _ in parts], axis=1),
            jnp.concatenate([rest for _, rest in parts], axis=1),
        ],
        axis=0,
    )
    found = product(picks, data).astype(jnp.int32)
    return found[:pairs] | (found[pairs:] << 16)


class Mail:
    def __init__(self, n_lat, n_lon):
        self.n_lat, self.n_lon = n_lat, n_lon
        self.n = n_lat * n_lon
        self.lat = lax.axis_index("lat")
        self.lon = lax.axis_index("lon")
        self.me = self.lat * n_lon + self.lon

    def split(self, i):
        if isinstance(i, int):
            return i // self.n_lon, i % self.n_lon
        return lax.div(i, self.n_lon), lax.rem(i, self.n_lon)

    def device(self, i):
        k, j = self.split(i)
        return lax.rem(self.lat + k, self.n_lat), lax.rem(self.lon + j, self.n_lon)

    def origin(self, i):
        k, j = self.split(i)
        return (
            lax.rem(self.lat - k + self.n_lat, self.n_lat),
            lax.rem(self.lon - j + self.n_lon, self.n_lon),
        )

    def number(self, device):
        return device[0] * self.n_lon + device[1]

    def greet(self):
        barrier = pltpu.get_barrier_semaphore()
        for i in range(1, self.n):
            pl.semaphore_signal(
                barrier, inc=1, device_id=self.device(i), device_id_type=pl.DeviceIdType.MESH
            )

    def meet(self):
        pl.semaphore_wait(pltpu.get_barrier_semaphore(), self.n - 1)


class Parcel:
    def __init__(self, mail, src, dst, rows, used, send, recv):
        self.mail, self.src, self.dst = mail, src, dst
        self.rows, self.used = rows, used
        self.send, self.recv = send, recv

    def part(self, ref, t):
        return ref.at[pl.ds(aligned(t * self.rows), self.used)]

    def copy(self, i, back=False):
        mail = self.mail
        device = mail.origin(i) if back else mail.device(i)
        return pltpu.make_async_remote_copy(
            src_ref=self.part(self.src, mail.number(device)),
            dst_ref=self.part(self.dst, mail.me),
            send_sem=self.send.at[i], recv_sem=self.recv.at[i],
            device_id=device, device_id_type=pl.DeviceIdType.MESH,
        )

    def own(self):
        me = self.mail.me
        return pltpu.make_async_copy(
            self.part(self.src, me), self.part(self.dst, me), self.send.at[0]
        )

    def post(self, order):
        for i in order:
            if i:
                self.copy(i).start()
            else:
                self.own().start()

    def collect(self, back=False):
        self.own().wait()
        for i in range(1, self.mail.n):
            self.copy(i, back).wait_recv()

    def settle(self, back=False):
        for i in range(1, self.mail.n):
            self.copy(i, back).wait_send()


def arrange(heads, room, plan):
    n = heads.shape[0]
    f32 = jnp.float32
    count = n * room
    spaces = plan.shape[1]
    tall = up8(MB + 1)

    def index(shape, dim):
        return lax.broadcasted_iota(jnp.int32, shape, dim)

    place = lax.rem(index((BLK, count), 1), room)
    spread = product(heads.astype(jnp.bfloat16), bits(index((BLK, count), 0) == place + SHIFT))
    entry = index((n, count), 1)
    mine = lax.div(entry, room) == index((n, count), 0)
    held = heads[:, SHIFT + room : SHIFT + room + 1]
    homes = jnp.where(lax.rem(entry, room).astype(f32) < held, spread, float(MB))
    homes = jnp.sum(jnp.where(mine, homes, 0.0), axis=0, keepdims=True).astype(jnp.int32)
    member = jnp.where(index((tall, count), 0) == homes, 1.0, 0.0)
    earlier = bits(index((count, count), 0) < index((count, count), 1))
    rank = product(member.astype(jnp.bfloat16), earlier)
    sizes = jnp.sum(member, axis=1, keepdims=True).astype(jnp.int32)
    sizes = (sizes + (BUNCH - 1)) // BUNCH * BUNCH
    sizes = jnp.where(index((tall, count), 0) < MB, sizes, 0)
    wide = sizes.astype(f32).astype(jnp.bfloat16)
    first = product(bits(index((tall, tall), 1) < index((tall, tall), 0)), wide)
    space = jnp.sum(member * (first + rank), axis=0, keepdims=True).astype(jnp.int32)
    space = jnp.where(homes < MB, space, -1)
    number = (index((8, count), 1) + 1).astype(f32).astype(jnp.bfloat16)
    found = lax.dot_general(
        number, bits(index((spaces, count), 0) == space),
        (((1,), (1,)), ((), ())), preferred_element_type=f32,
    )
    plan[...] = found.astype(jnp.int32)
    ends = first.astype(jnp.int32)[:MB, :BLK] + sizes[:MB, :BLK]
    over = jnp.where(ends <= BUNCH * index((MB, BLK), 1), 1, 0)
    plan[1:2, 0:BLK] = jnp.sum(over, axis=0, keepdims=True)
    plan[2:3, 0:BLK] = jnp.max(ends, axis=0, keepdims=True)


def advect_kernel(
    dims, slots, targets, requests, *refs,
):
    far = refs[:6]
    moved, turbulence, heights, shares, plan = refs[6:11]
    positions, velocity, increments, mass, keys, tiles = near = refs[11:17]
    advect(
        dims, slots, targets, requests, far, near, positions, velocity, increments, mass, keys,
        tiles, moved, turbulence, heights, shares, plan, *refs[17:],
    )


def advect(
    dims, slots, targets, requests, far, near, positions, velocity, increments, mass, keys, tiles,
    moved, turbulence, heights, shares, plan,
    spot_msg, spots, back_msg, winds, mass_msg, z_msg,
    table, places, sorted_spots, sorted_mass, own_heads, heads, scaled, parts, found, sorted_z,
    asked_of, place, spot_sems, back_sems, mass_sems, z_sems, local,
):
    n_lat, n_lon, blocks, room, spot_rows, back_rows, mass_rows, z_rows = dims
    mail = Mail(n_lat, n_lon)
    mail.greet()
    fetches = [
        pltpu.make_async_copy(far[i], near[i], local.at[2 + i]) for i in (0, 4, 3, 5, 1, 2)
    ]
    for copy in fetches:
        copy.start()
    n = mail.n
    entries = Q * room
    half = entries // 2
    few = room // 2
    f32 = jnp.float32
    bf16 = jnp.bfloat16
    rows = lax.broadcasted_iota(jnp.int32, (blocks, blocks), 0)
    cols = lax.broadcasted_iota(jnp.int32, (blocks, blocks), 1)
    tile_ids = lax.broadcasted_iota(jnp.int32, (n, blocks), 0)
    lanes = lax.broadcasted_iota(jnp.int32, (blocks, BLK), 1)
    slot_row = slots[...]
    dest_row = targets[...]
    table[...] = jnp.zeros_like(table)
    table[0:1, :] = slot_row.astype(f32)
    table[1:2, :] = dest_row.astype(f32)
    table[2:4, 0:n] = requests[...].astype(f32)
    turned = table[...].T
    slot_col = turned[:, 0:1].astype(jnp.int32)
    dest_col = turned[:, 1:2].astype(jnp.int32)
    same_slot = jnp.where((slot_col == slot_row) & (rows < cols), 1.0, 0.0)
    slot_rank = jnp.sum(same_slot, axis=0, keepdims=True).astype(jnp.int32)
    same_dest = jnp.where((dest_col == dest_row) & (rows < cols), 1.0, 0.0)
    dest_rank = jnp.sum(same_dest, axis=0, keepdims=True).astype(jnp.int32)
    entry = (slot_row & 1) * room + slot_rank
    places[...] = jnp.zeros_like(places)
    places[0:1, :] = (((slot_row >> 1) * back_rows + (entry >> 1)) << 1) | (entry & 1)

    fetches[0].wait()
    words = chosen(
        chooser(slot_row * room + slot_rank, n * half),
        [
            code(positions[0], FULL / (BY - 1)),
            code(positions[1], FULL / (BX - 1)),
            code(positions[2], FULL / (LEV - 1)),
        ],
    )
    for c in range(3):
        sorted_spots[c] = words[:, c * BLK : (c + 1) * BLK]
    counts = product(bits((slot_row >> 1) == tile_ids), bits(lanes == (slot_col & 1)))
    asked = turned[0:n] if n < BLK else turned
    front = lanes[0:n]
    before = bits((dest_col == dest_row) & (cols < rows))
    rank_col = product(before, jnp.ones((blocks, BLK), bf16)).astype(jnp.int32)
    fetches[1].wait()
    homes = jnp.where(lanes == SHIFT + rank_col, (keys[...] >> 7).astype(f32), 0.0)
    homes = jnp.where(lanes == SHIFT + room, 1.0, homes).astype(bf16)
    landing = product(bits(dest_row == tile_ids), homes)
    counts = jnp.where((front == 2) | (front == 3), asked, counts)
    own_heads[...] = (counts + landing).astype(jnp.int32)

    def address(t, carry):
        for c in range(3):
            spot_msg[pl.ds(t * spot_rows + c * half, half), :] = sorted_spots[
                c, pl.ds(t * half, half), :
            ]
        spot_msg[pl.ds(t * spot_rows + 3 * half, 1), :] = own_heads[pl.ds(t, 1), :]
        return carry

    lax.fori_loop(0, n, address, 0, unroll=8)
    spot_mail = Parcel(
        mail, spot_msg, spots, spot_rows, 3 * half + 1, spot_sems.at[0], spot_sems.at[1]
    )
    back_mail = Parcel(mail, back_msg, winds, back_rows, 3 * half, back_sems.at[0], back_sems.at[1])
    mass_mail = Parcel(
        mail, mass_msg, shares, mass_rows, (S + 1) * few, mass_sems.at[0], mass_sems.at[1]
    )
    z_mail = Parcel(mail, z_msg, heights, z_rows, few, z_sems.at[0], z_sems.at[1])
    dest_place = dest_row * room + dest_rank
    picks = chooser(dest_place, n * few)
    fetches[2].wait()
    for s in range(0, S, 2):
        words = chosen(picks, [code(mass[pl.ds(s + i, blocks, stride=S), :], FULL) for i in range(2)])
        for i in range(2):
            sorted_mass[s + i] = words[:, i * BLK : (i + 1) * BLK]
    sorted_mass[S] = chosen(picks, [keys[...]])

    def wrap_mass(t, carry):
        for s in range(S + 1):
            mass_msg[pl.ds(t * mass_rows + s * few, few), :] = sorted_mass[s, pl.ds(t * few, few), :]
        return carry

    lax.fori_loop(0, n, wrap_mass, 0, unroll=4)
    order = list(range(n))
    lats = [order[k * n_lon : (k + 1) * n_lon] for k in range(n_lat)]
    mail.meet()
    spot_mail.post(order)
    placing = pltpu.make_async_copy(places, place, local.at[1])
    placing.start()

    mass_mail.post(lats[0])
    mass_mail.post(lats[1])
    for copy in fetches[3:]:
        copy.wait()
    for c in range(3):
        turbulence[c] = DECAY * velocity[c] + KICK * increments[c]

    levels = lax.broadcasted_iota(jnp.int32, (LEV, BLK), 0).astype(f32)
    xs_at = lax.broadcasted_iota(jnp.int32, (BX, BLK), 0).astype(f32)
    ys_at = lax.broadcasted_iota(jnp.int32, (BY, BLK), 0).astype(f32)

    def asking(i):
        row = mail.number(mail.origin(i)) * spot_rows + 3 * half
        return pltpu.make_async_copy(
            spots.at[pl.ds(aligned(row) if half % 8 == 0 else row, 1)], asked_of, local.at[0]
        )

    def weights(y, x):
        hy = hat(y - ys_at)
        hx = hat(x - xs_at)
        flat = jnp.concatenate([hy[i : i + 1] * hx for i in range(BY)], axis=0)
        flat_hi = flat.astype(bf16)
        flat_lo = (flat - flat_hi.astype(f32)).astype(bf16)
        return jnp.concatenate([flat_hi, flat_lo], axis=0)

    def interpolate(i, mets):
        o = mail.number(mail.origin(i))
        base = o * spot_rows
        for c, top in enumerate((BY - 1, BX - 1, LEV - 1)):
            word = spots[pl.ds(base + c * half, half), :]
            scaled[c] = low(word) * (top / FULL)
            scaled[3 + c] = high(word) * (top / FULL)
        for k in range(half):
            block = tiles[mets[k // few]]
            seen = product(
                jnp.concatenate([block, block], axis=1),
                jnp.concatenate(
                    [
                        weights(scaled[3 * side, k : k + 1, :], scaled[3 * side + 1, k : k + 1, :])
                        for side in range(2)
                    ],
                    axis=1,
                ),
            )
            for side in range(2):
                wz = hat(scaled[3 * side + 2, k : k + 1, :] - levels).astype(bf16).astype(f32)
                for c in range(3):
                    part = seen[c * LEV : (c + 1) * LEV, side * BLK : (side + 1) * BLK] * wz
                    total = part[0:8]
                    for v in range(8, LEV, 8):
                        total = total + part[v : v + 8]
                    parts[3 * side + c, 8 * k : 8 * k + 8, :] = total
        for c in range(3):
            codes = []
            for side in range(2):
                wind = parts[3 * side + c, pl.ds(0, half, stride=8), :]
                for v in range(1, 8):
                    wind = wind + parts[3 * side + c, pl.ds(v, half, stride=8), :]
                codes.append(code(wind + GUST, FULL / (2 * GUST)))
            back_msg[pl.ds(o * back_rows + c * half, half), :] = codes[0] | (codes[1] << 16)

    spot_mail.own().wait()
    asking(0).start()
    asking(0).wait()

    def serve(i, carry):
        mets = [jnp.clip(asked_of[0, 2 + k], 0, MB - 1) for k in range(Q)]

        @pl.when(i + 1 < n)
        def _():
            spot_mail.copy(i + 1).wait_recv()
            asking(i + 1).start()

        interpolate(i, mets)

        @pl.when(i > 0)
        def _():
            back_mail.copy(i, back=True).start()

        @pl.when(i == 0)
        def _():
            back_mail.own().start()

        @pl.when(i + 1 < n)
        def _():
            asking(i + 1).wait()

        return carry

    lax.fori_loop(0, n, serve, 0)
    for o in range(n):
        row = o * spot_rows + 3 * half
        heads[o : o + 1, :] = spots[row : row + 1, :]
    arrange(heads[...].astype(f32), room, plan)
    mass_mail.post(lats[3])
    placing.wait()
    back_mail.collect()

    def fetch(b, carry):
        spot = place[0, b]
        row = jnp.clip(spot >> 1, 0, n * back_rows - 2 * half - 1)
        odd = 16 * (spot & 1)
        for c in range(3):
            word = winds[pl.ds(row + c * half, 1), :]
            found[c, pl.ds(b, 1), :] = lax.shift_right_logical(word, jnp.full_like(word, odd))
        return carry

    lax.fori_loop(0, blocks, fetch, 0, unroll=8)
    for c, top in enumerate((BY - 1.0, BX - 1.0, LEV - 1.0)):
        wind = low(found[c]) * (2 * GUST / FULL) - GUST
        moved[c] = jnp.clip(positions[c] + STEP * (wind + turbulence[c]), 0.0, top)
    sorted_z[...] = chosen(picks, [code(moved[2], FULL / (LEV - 1))])

    def wrap(t, carry):
        z_msg[pl.ds(t * z_rows, few), :] = sorted_z[pl.ds(t * few, few), :]
        return carry

    lax.fori_loop(0, n, wrap, 0, unroll=8)
    z_mail.post(order)
    mass_mail.post(lats[2])
    z_mail.collect()
    mass_mail.collect()
    spot_mail.settle()
    back_mail.settle()
    mass_mail.settle()
    z_mail.settle()


def deposit_kernel(
    dims, plan, heights, shares, moved_in, turbulence_in,
    moved, turbulence, out,
    total, made, moved_held, turbulence_held, columns, sems,
):
    room, mass_rows, z_rows = dims
    few = room // 2
    into = [
        pltpu.make_async_copy(moved_in, moved_held, sems.at[0]),
        pltpu.make_async_copy(turbulence_in, turbulence_held, sems.at[1]),
    ]
    onward = [
        pltpu.make_async_copy(moved_held, moved, sems.at[2]),
        pltpu.make_async_copy(turbulence_held, turbulence, sems.at[3]),
    ]
    for copy in into:
        copy.start()
    levels = lax.broadcasted_iota(jnp.int32, (SPAN, BLK), 0).astype(jnp.float32)
    columns[...] = lax.broadcasted_iota(jnp.int32, (2 * MBC, BLK), 0)

    def clear(h, carry):
        total[h] = jnp.zeros((S * SPAN, 2 * MBC), jnp.float32)
        return carry

    lax.fori_loop(0, MB, clear, 0)

    def operands(number):
        entry = jnp.maximum(number - 1, 0)
        o = lax.div(entry, room)
        q = lax.rem(entry, room)
        base = o * mass_rows + (q >> 1)
        odd = 16 * (q & 1)

        def half_of(word):
            return lax.shift_right_logical(word, jnp.full_like(word, odd))

        key = half_of(shares[pl.ds(base + S * few, 1), :]) & (MBC - 1)
        z = low(half_of(heights[pl.ds(o * z_rows + (q >> 1), 1), :])) * ((LEV - 1) / FULL)
        upper = z >= SPLIT
        z = z - jnp.where(upper, float(SPLIT), 0.0)
        key = key + jnp.where(upper, MBC, 0) + jnp.where(number > 0, 0, 4 * MBC)
        vert = hat(z - levels)
        parts = low(half_of(shares[pl.ds(base, S, stride=few), :])) * (1 / FULL)
        weights = jnp.concatenate([parts[s : s + 1] * vert for s in range(S)], axis=0)
        return weights.astype(jnp.bfloat16), bits(key == columns[...])

    def multiply(c):
        h = jnp.minimum(plan[1, c], MB - 1)
        pairs = [operands(plan[0, c * BUNCH + j]) for j in range(BUNCH)]
        total[h] += lax.dot_general(
            jnp.concatenate([w for w, _ in pairs], axis=1),
            jnp.concatenate([p for _, p in pairs], axis=1),
            (((1,), (1,)), ((), ())),
            preferred_element_type=jnp.float32,
        )

    def several(i, carry):
        for j in range(CHUNKS):
            multiply(CHUNKS * i + j)
        return carry

    chunks = plan[2, 0] // BUNCH
    lax.fori_loop(0, (chunks + CHUNKS - 1) // CHUNKS, several, 0)
    for copy in into:
        copy.wait()
    for copy in onward:
        copy.start()

    def leave(h):
        return pltpu.make_async_copy(made.at[h], out.at[h], sems.at[4 + h])

    def finish(h, carry):
        for s in range(S):
            low_part = total[h, s * SPAN : (s + 1) * SPAN, 0:MBC]
            high_part = total[h, s * SPAN : (s + 1) * SPAN, MBC : 2 * MBC]
            shared = SPAN - SPLIT
            made[h, s * LEV : s * LEV + SPLIT, :] = low_part[:SPLIT]
            made[h, s * LEV + SPLIT : s * LEV + SPAN, :] = low_part[SPLIT:] + high_part[:shared]
            made[h, s * LEV + SPAN : (s + 1) * LEV, :] = high_part[shared:]
        leave(h).start()
        return carry

    lax.fori_loop(0, MB, finish, 0)
    for copy in onward:
        copy.wait()
    for h in range(MB):
        leave(h).wait()


def body(
    winds, positions, velocity, increments, mass, requests, block_slots, destinations, cell_keys
):
    n_lat = lax.axis_size("lat")
    n_lon = lax.axis_size("lon")
    n = n_lat * n_lon
    blocks = positions.shape[0]
    room = 2 * blocks // n
    half = Q * room // 2
    few = room // 2
    spot_rows = up8(3 * half + 1)
    back_rows = up8(3 * half)
    mass_rows = up8((S + 1) * few)
    z_rows = up8(few)
    spaces = -(-(n * room + (MB + CHUNKS) * BUNCH) // BLK) * BLK
    i32 = jnp.int32
    f32 = jnp.float32
    like = jax.ShapeDtypeStruct
    dma = pltpu.SemaphoreType.DMA

    anywhere = pl.BlockSpec(memory_space=pl.ANY)
    mass = mass.reshape(-1, BLK)
    winds = winds.reshape(MB, 3 * LEV, MBC)
    positions, velocity, increments = (
        each.transpose(1, 0, 2) for each in (positions, velocity, increments)
    )
    moved, turbulence, heights, shares, plan = pl.pallas_call(
        functools.partial(
            advect_kernel,
            (n_lat, n_lon, blocks, room, spot_rows, back_rows, mass_rows, z_rows),
        ),
        out_shape=(
            like(positions.shape, f32),
            like(positions.shape, f32),
            like((n * z_rows, BLK), i32),
            like((n * mass_rows, BLK), i32),
            like((8, spaces), i32),
        ),
        in_specs=[VMEM] * 3 + [anywhere] * 6,
        out_specs=(VMEM,) * 5,
        scratch_shapes=[
            pltpu.VMEM(each.shape, each.dtype)
            for each in (positions, velocity, increments, mass, cell_keys, winds)
        ]
        + [
            pltpu.VMEM((n * spot_rows, BLK), i32),
            pltpu.VMEM((n * spot_rows, BLK), i32),
            pltpu.VMEM((n * back_rows, BLK), i32),
            pltpu.VMEM((n * back_rows, BLK), i32),
            pltpu.VMEM((n * mass_rows, BLK), i32),
            pltpu.VMEM((n * z_rows, BLK), i32),
            pltpu.VMEM((BLK, BLK), f32),
            pltpu.VMEM((8, blocks), i32),
            pltpu.VMEM((3, n * half, BLK), i32),
            pltpu.VMEM((S + 1, n * few, BLK), i32),
            pltpu.VMEM((n, BLK), i32),
            pltpu.VMEM((n, BLK), i32),
            pltpu.VMEM((6, half, BLK), f32),
            pltpu.VMEM((6, 8 * half, BLK), f32),
            pltpu.VMEM((3, blocks, BLK), i32),
            pltpu.VMEM((n * few, BLK), i32),
            pltpu.SMEM((1, BLK), i32),
            pltpu.SMEM((8, blocks), i32),
            dma((2, n)),
            dma((2, n)),
            dma((2, n)),
            dma((2, n)),
            dma((8,)),
        ],
        compiler_params=pltpu.CompilerParams(collective_id=0, has_side_effects=True),
        name="advect",
    )(
        block_slots.reshape(1, -1), destinations.reshape(1, -1), requests[0].T,
        positions, velocity, increments, mass, cell_keys, winds,
    )
    moved, turbulence, total = pl.pallas_call(
        functools.partial(deposit_kernel, (room, mass_rows, z_rows)),
        out_shape=(
            like(positions.shape, f32),
            like(positions.shape, f32),
            like((MB, S * LEV, MBC), f32),
        ),
        in_specs=[SMEM, VMEM, VMEM, anywhere, anywhere],
        out_specs=(anywhere,) * 3,
        scratch_shapes=[
            pltpu.VMEM((MB, S * SPAN, 2 * MBC), f32),
            pltpu.VMEM((MB, S * LEV, MBC), f32),
            pltpu.VMEM(positions.shape, f32),
            pltpu.VMEM(positions.shape, f32),
            pltpu.VMEM((2 * MBC, BLK), i32),
            dma((4 + MB,)),
        ],
        name="deposit",
    )(plan, heights, shares, moved, turbulence)
    concentration = total.reshape(MBR, MBK, S, LEV, MBC)
    return (moved.transpose(1, 0, 2), turbulence.transpose(1, 0, 2), concentration)


def solution(mesh):
    rows = ("lat", "lon")
    in_specs = (
        P("lat", "lon", None, None, None),
        P(rows, None, None),
        P(rows, None, None),
        P(rows, None, None),
        P(rows, None, None),
        P(rows, None, None),
        P(rows, None),
        P(rows, None),
        P(rows, None),
    )
    out_specs = (
        P(rows, None, None),
        P(rows, None, None),
        P("lat", "lon", None, None, None),
    )
    return jax.shard_map(body, mesh=mesh, in_specs=in_specs, out_specs=out_specs, check_vma=False)
```

profile of v0, /device:TPU:1, one launch (start us, length us, event | category | flops | bytes accessed | tf_op | source)
XLA Modules:
  0.0 56.9 jit_solution(12675624149054146170)
XLA Ops:
  0.6 44.6 %advect.1 = (f32[3,128,128]{2,1,0:T(8,128)}, f32[3,128,128]{2,1,0:T(8,128)}, s32[256,128]{1,0:T(8,128)}, s32[1280,128]{1,0:T(8,128)}, s32[8,384]{1,0:T(8,128)}) custom-call(s32[1,128]{1,0:T(1,128)} %bitcast.19, s32[1,128]{1,0:T(1,128)} %bitcast.20, s32[2,32]{1,0:T(2,128)} %bitcast.18, f32[3,128,128]{2,1,0:T(8,128)} %bitcast.15, f32[3,128,128]{2,1,0:T(8,128)} %bitcast.16, ...), custom_call_target="tpu_custom_call" | custom-call | tf_op jit(solution)/shard_map/advect/pallas_call | solution.py:573
  45.2 11.6 %deposit.1 = (f32[3,128,128]{2,1,0:T(8,128)}, f32[3,128,128]{2,1,0:T(8,128)}, f32[16,320,128]{2,1,0:T(8,128)}) custom-call(s32[8,384]{1,0:T(8,128)} %get-tuple-element.11.plan, s32[256,128]{1,0:T(8,128)} %get-tuple-element.12.heights, s32[1280,128]{1,0:T(8,128)} %get-tuple-element.13.shares, f32[3,128,128]{2,1,0:T(8,128)} %get-tuple-element.14.moved_in, ...), custom_call_target="tpu_custom_call" | custom-call | tf_op jit(solution)/shard_map/deposit/pallas_call | solution.py:622
where the time goes:
time: 57.7 us; the launch traced here: 56.9 us
  Pallas kernels  56.2 us (97%)
  between operations  0.64 us (1%)
    pallas_call x1, Pallas kernels, body(): pl.pallas_call(functools.partial(advect_kernel, (n_lat, n_lon, blocks, ro...  44.6 us
    pallas_call x1, Pallas kernels, body(): pl.pallas_call(functools.partial(deposit_kernel, (room, mass_rows, z_rows...  11.6 us

commit v1 on v0

--- a/solution.py
+++ b/solution.py
@@ -26,7 +26,7 @@
 GUST = 6.1
 BUNCH = 4
 SHIFT = 64
-CHUNKS = 4
+CHUNKS = 6
 SPLIT = 16
 SPAN = LEV - SPLIT
 VMEM = pl.BlockSpec(memory_space=pltpu.VMEM)
@@ -211,21 +211,20 @@
     plan[2:3, 0:BLK] = jnp.max(ends, axis=0, keepdims=True)
 
 
-def advect_kernel(
-    dims, slots, targets, requests, *refs,
-):
-    far = refs[:6]
-    moved, turbulence, heights, shares, plan = refs[6:11]
-    positions, velocity, increments, mass, keys, tiles = near = refs[11:17]
+def advect_kernel(dims, *refs):
+    far = refs[:9]
+    gone, heights, shares, plan = refs[9:11], *refs[11:14]
+    near = refs[14:23]
+    slots, targets, requests, positions, velocity, increments, mass, keys, tiles = near
     advect(
-        dims, slots, targets, requests, far, near, positions, velocity, increments, mass, keys,
-        tiles, moved, turbulence, heights, shares, plan, *refs[17:],
+        dims, far, near, gone, slots, targets, requests, positions, velocity, increments, mass,
+        keys, tiles, heights, shares, plan, *refs[23:],
     )
 
 
 def advect(
-    dims, slots, targets, requests, far, near, positions, velocity, increments, mass, keys, tiles,
-    moved, turbulence, heights, shares, plan,
+    dims, far, near, gone, slots, targets, requests, positions, velocity, increments, mass,
+    keys, tiles, heights, shares, plan, moved, turbulence,
     spot_msg, spots, back_msg, winds, mass_msg, z_msg,
     table, places, sorted_spots, sorted_mass, own_heads, heads, scaled, parts, found, sorted_z,
     asked_of, place, spot_sems, back_sems, mass_sems, z_sems, local,
@@ -234,10 +233,13 @@
     mail = Mail(n_lat, n_lon)
     mail.greet()
     fetches = [
-        pltpu.make_async_copy(far[i], near[i], local.at[2 + i]) for i in (0, 4, 3, 5, 1, 2)
+        pltpu.make_async_copy(far[i], near[i], local.at[2 + i])
+        for i in (0, 1, 2, 3, 7, 6, 8, 4, 5)
     ]
     for copy in fetches:
         copy.start()
+    for copy in fetches[:3]:
+        copy.wait()
     n = mail.n
     entries = Q * room
     half = entries // 2
@@ -265,7 +267,7 @@
     places[...] = jnp.zeros_like(places)
     places[0:1, :] = (((slot_row >> 1) * back_rows + (entry >> 1)) << 1) | (entry & 1)
 
-    fetches[0].wait()
+    fetches[3].wait()
     words = chosen(
         chooser(slot_row * room + slot_rank, n * half),
         [
@@ -281,7 +283,7 @@
     front = lanes[0:n]
     before = bits((dest_col == dest_row) & (cols < rows))
     rank_col = product(before, jnp.ones((blocks, BLK), bf16)).astype(jnp.int32)
-    fetches[1].wait()
+    fetches[4].wait()
     homes = jnp.where(lanes == SHIFT + rank_col, (keys[...] >> 7).astype(f32), 0.0)
     homes = jnp.where(lanes == SHIFT + room, 1.0, homes).astype(bf16)
     landing = product(bits(dest_row == tile_ids), homes)
@@ -307,7 +309,7 @@
     z_mail = Parcel(mail, z_msg, heights, z_rows, few, z_sems.at[0], z_sems.at[1])
     dest_place = dest_row * room + dest_rank
     picks = chooser(dest_place, n * few)
-    fetches[2].wait()
+    fetches[5].wait()
     for s in range(0, S, 2):
         words = chosen(picks, [code(mass[pl.ds(s + i, blocks, stride=S), :], FULL) for i in range(2)])
         for i in range(2):
@@ -329,7 +331,7 @@
 
     mass_mail.post(lats[0])
     mass_mail.post(lats[1])
-    for copy in fetches[3:]:
+    for copy in fetches[6:]:
         copy.wait()
     for c in range(3):
         turbulence[c] = DECAY * velocity[c] + KICK * increments[c]
@@ -446,7 +448,15 @@
 
     lax.fori_loop(0, n, wrap, 0, unroll=8)
     z_mail.post(order)
+    leaving = [
+        pltpu.make_async_copy(held, gone[i], local.at[2 + i])
+        for i, held in enumerate((moved, turbulence))
+    ]
+    for copy in leaving:
+        copy.start()
     mass_mail.post(lats[2])
+    for copy in leaving:
+        copy.wait()
     z_mail.collect()
     mass_mail.collect()
     spot_mail.settle()
@@ -456,9 +466,9 @@
 
 
 def deposit_kernel(
-    dims, plan, heights, shares, moved_in, turbulence_in,
+    dims, plan, heights_in, shares_in, moved_in, turbulence_in,
     moved, turbulence, out,
-    total, made, moved_held, turbulence_held, columns, sems,
+    heights, shares, made, moved_held, turbulence_held, columns, sems,
 ):
     room, mass_rows, z_rows = dims
     few = room // 2
@@ -470,16 +480,22 @@
         pltpu.make_async_copy(moved_held, moved, sems.at[2]),
         pltpu.make_async_copy(turbulence_held, turbulence, sems.at[3]),
     ]
-    for copy in into:
+    stock = [
+        pltpu.make_async_copy(shares_in, shares, sems.at[4 + MB]),
+        pltpu.make_async_copy(heights_in, heights, sems.at[5 + MB]),
+    ]
+    for copy in stock + into:
         copy.start()
     levels = lax.broadcasted_iota(jnp.int32, (SPAN, BLK), 0).astype(jnp.float32)
     columns[...] = lax.broadcasted_iota(jnp.int32, (2 * MBC, BLK), 0)
 
     def clear(h, carry):
-        total[h] = jnp.zeros((S * SPAN, 2 * MBC), jnp.float32)
+        made[h] = jnp.zeros((S * LEV, MBC), jnp.float32)
         return carry
 
     lax.fori_loop(0, MB, clear, 0)
+    for copy in stock:
+        copy.wait()
 
     def operands(number):
         entry = jnp.maximum(number - 1, 0)
@@ -504,12 +520,19 @@
     def multiply(c):
         h = jnp.minimum(plan[1, c], MB - 1)
         pairs = [operands(plan[0, c * BUNCH + j]) for j in range(BUNCH)]
-        total[h] += lax.dot_general(
+        found = lax.dot_general(
             jnp.concatenate([w for w, _ in pairs], axis=1),
             jnp.concatenate([p for _, p in pairs], axis=1),
             (((1,), (1,)), ((), ())),
             preferred_element_type=jnp.float32,
         )
+        shared = SPAN - SPLIT
+        for s in range(S):
+            low_part = found[s * SPAN : (s + 1) * SPAN, 0:MBC]
+            high_part = found[s * SPAN : (s + 1) * SPAN, MBC : 2 * MBC]
+            made[h, s * LEV : s * LEV + SPLIT, :] += low_part[:SPLIT]
+            made[h, s * LEV + SPLIT : s * LEV + SPAN, :] += low_part[SPLIT:] + high_part[:shared]
+            made[h, s * LEV + SPAN : (s + 1) * LEV, :] += high_part[shared:]
 
     def several(i, carry):
         for j in range(CHUNKS):
@@ -526,18 +549,8 @@
     def leave(h):
         return pltpu.make_async_copy(made.at[h], out.at[h], sems.at[4 + h])
 
-    def finish(h, carry):
-        for s in range(S):
-            low_part = total[h, s * SPAN : (s + 1) * SPAN, 0:MBC]
-            high_part = total[h, s * SPAN : (s + 1) * SPAN, MBC : 2 * MBC]
-            shared = SPAN - SPLIT
-            made[h, s * LEV : s * LEV + SPLIT, :] = low_part[:SPLIT]
-            made[h, s * LEV + SPLIT : s * LEV + SPAN, :] = low_part[SPLIT:] + high_part[:shared]
-            made[h, s * LEV + SPAN : (s + 1) * LEV, :] = high_part[shared:]
+    for h in range(MB):
         leave(h).start()
-        return carry
-
-    lax.fori_loop(0, MB, finish, 0)
     for copy in onward:
         copy.wait()
     for h in range(MB):
@@ -570,6 +583,10 @@
     positions, velocity, increments = (
         each.transpose(1, 0, 2) for each in (positions, velocity, increments)
     )
+    inputs = (
+        block_slots.reshape(1, -1), destinations.reshape(1, -1), requests[0].T,
+        positions, velocity, increments, mass, cell_keys, winds,
+    )
     moved, turbulence, heights, shares, plan = pl.pallas_call(
         functools.partial(
             advect_kernel,
@@ -582,11 +599,11 @@
             like((n * mass_rows, BLK), i32),
             like((8, spaces), i32),
         ),
-        in_specs=[VMEM] * 3 + [anywhere] * 6,
-        out_specs=(VMEM,) * 5,
+        in_specs=[pl.BlockSpec(memory_space=pltpu.HBM)] * 9,
+        out_specs=(anywhere,) * 4 + (VMEM,),
         scratch_shapes=[
             pltpu.VMEM(each.shape, each.dtype)
-            for each in (positions, velocity, increments, mass, cell_keys, winds)
+            for each in inputs + (positions, positions)
         ]
         + [
             pltpu.VMEM((n * spot_rows, BLK), i32),
@@ -611,14 +628,11 @@
             dma((2, n)),
             dma((2, n)),
             dma((2, n)),
-            dma((8,)),
+            dma((2 + len(inputs),)),
         ],
         compiler_params=pltpu.CompilerParams(collective_id=0, has_side_effects=True),
         name="advect",
-    )(
-        block_slots.reshape(1, -1), destinations.reshape(1, -1), requests[0].T,
-        positions, velocity, increments, mass, cell_keys, winds,
-    )
+    )(*inputs)
     moved, turbulence, total = pl.pallas_call(
         functools.partial(deposit_kernel, (room, mass_rows, z_rows)),
         out_shape=(
@@ -626,15 +640,16 @@
             like(positions.shape, f32),
             like((MB, S * LEV, MBC), f32),
         ),
-        in_specs=[SMEM, VMEM, VMEM, anywhere, anywhere],
+        in_specs=[SMEM] + [anywhere] * 4,
         out_specs=(anywhere,) * 3,
         scratch_shapes=[
-            pltpu.VMEM((MB, S * SPAN, 2 * MBC), f32),
+            pltpu.VMEM(heights.shape, i32),
+            pltpu.VMEM(shares.shape, i32),
             pltpu.VMEM((MB, S * LEV, MBC), f32),
             pltpu.VMEM(positions.shape, f32),
             pltpu.VMEM(positions.shape, f32),
             pltpu.VMEM((2 * MBC, BLK), i32),
-            dma((4 + MB,)),
+            dma((6 + MB,)),
         ],
         name="deposit",
     )(plan, heights, shares, moved, turbulence)

time: 57.7 us -> 56.1 us (0.972)
  the two profiles are of different devices: /device:TPU:1 before, /device:TPU:28 now
where the time goes in v1:
time: 56.1 us; the launch traced here: 55.5 us
  Pallas kernels  54.8 us (98%)
  between operations  0.64 us (1%)
    pallas_call x1, Pallas kernels, body(): pl.pallas_call(functools.partial(advect_kernel, (n_lat, n_lon, blocks, ro...  43 us
    pallas_call x1, Pallas kernels, body(): pl.pallas_call(functools.partial(deposit_kernel, (room, mass_rows, z_rows...  11.8 us

profile of v1, /device:TPU:28, one launch (start us, length us, event | category | flops | bytes accessed | tf_op | source)
XLA Modules:
  0.0 55.5 jit_solution(11881914393342466707)
XLA Ops:
  0.6 43.0 %advect.1 = (f32[3,128,128]{2,1,0:T(8,128)}, f32[3,128,128]{2,1,0:T(8,128)}, s32[256,128]{1,0:T(8,128)}, s32[1280,128]{1,0:T(8,128)}, s32[8,384]{1,0:T(8,128)}) custom-call(s32[1,128]{1,0:T(1,128)} %bitcast.19, s32[1,128]{1,0:T(1,128)} %bitcast.20, s32[2,32]{1,0:T(2,128)} %bitcast.18, f32[3,128,128]{2,1,0:T(8,128)} %bitcast.15, f32[3,128,128]{2,1,0:T(8,128)} %bitcast.16, ...), custom_call_target="tpu_custom_call" | custom-call | tf_op jit(solution)/shard_map/advect/pallas_call | solution.py:590
  43.7 11.8 %deposit.1 = (f32[3,128,128]{2,1,0:T(8,128)}, f32[3,128,128]{2,1,0:T(8,128)}, f32[16,320,128]{2,1,0:T(8,128)}) custom-call(s32[8,384]{1,0:T(8,128)} %get-tuple-element.11.plan, s32[256,128]{1,0:T(8,128)} %get-tuple-element.12.heights_in, s32[1280,128]{1,0:T(8,128)} %get-tuple-element.13.shares_in, f32[3,128,128]{2,1,0:T(8,128)} %get-tuple-element.14.moved_in, ...), custom_call_target="tpu_custom_call" | custom-call | tf_op jit(solution)/shard_map/deposit/pallas_call | solution.py:636

commit v2 on v1

--- a/solution.py
+++ b/solution.py
@@ -213,18 +213,19 @@
 
 def advect_kernel(dims, *refs):
     far = refs[:9]
-    gone, heights, shares, plan = refs[9:11], *refs[11:14]
+    gone = (refs[9], refs[10], refs[13])
+    heights, shares = refs[11:13]
     near = refs[14:23]
     slots, targets, requests, positions, velocity, increments, mass, keys, tiles = near
     advect(
         dims, far, near, gone, slots, targets, requests, positions, velocity, increments, mass,
-        keys, tiles, heights, shares, plan, *refs[23:],
+        keys, tiles, heights, shares, *refs[23:],
     )
 
 
 def advect(
     dims, far, near, gone, slots, targets, requests, positions, velocity, increments, mass,
-    keys, tiles, heights, shares, plan, moved, turbulence,
+    keys, tiles, heights, shares, moved, turbulence, plan,
     spot_msg, spots, back_msg, winds, mass_msg, z_msg,
     table, places, sorted_spots, sorted_mass, own_heads, heads, scaled, parts, found, sorted_z,
     asked_of, place, spot_sems, back_sems, mass_sems, z_sems, local,
@@ -450,7 +451,7 @@
     z_mail.post(order)
     leaving = [
         pltpu.make_async_copy(held, gone[i], local.at[2 + i])
-        for i, held in enumerate((moved, turbulence))
+        for i, held in enumerate((moved, turbulence, plan))
     ]
     for copy in leaving:
         copy.start()
@@ -466,9 +467,9 @@
 
 
 def deposit_kernel(
-    dims, plan, heights_in, shares_in, moved_in, turbulence_in,
+    dims, plan_in, heights_in, shares_in, moved_in, turbulence_in,
     moved, turbulence, out,
-    heights, shares, made, moved_held, turbulence_held, columns, sems,
+    plan, heights, shares, made, moved_held, turbulence_held, columns, sems,
 ):
     room, mass_rows, z_rows = dims
     few = room // 2
@@ -483,6 +484,7 @@
     stock = [
         pltpu.make_async_copy(shares_in, shares, sems.at[4 + MB]),
         pltpu.make_async_copy(heights_in, heights, sems.at[5 + MB]),
+        pltpu.make_async_copy(plan_in, plan, sems.at[6 + MB]),
     ]
     for copy in stock + into:
         copy.start()
@@ -534,23 +536,27 @@
             made[h, s * LEV + SPLIT : s * LEV + SPAN, :] += low_part[SPLIT:] + high_part[:shared]
             made[h, s * LEV + SPAN : (s + 1) * LEV, :] += high_part[shared:]
 
-    def several(i, carry):
+    def leave(h):
+        return pltpu.make_async_copy(made.at[h], out.at[h], sems.at[4 + h])
+
+    def release(h, carry):
+        leave(h).start()
+        return carry
+
+    def several(i, ready):
         for j in range(CHUNKS):
             multiply(CHUNKS * i + j)
-        return carry
-
-    chunks = plan[2, 0] // BUNCH
-    lax.fori_loop(0, (chunks + CHUNKS - 1) // CHUNKS, several, 0)
+        done = jnp.minimum(plan[1, CHUNKS * (i + 1)], MB)
+        lax.fori_loop(ready, done, release, 0)
+        return jnp.maximum(ready, done)
+
     for copy in into:
         copy.wait()
     for copy in onward:
         copy.start()
-
-    def leave(h):
-        return pltpu.make_async_copy(made.at[h], out.at[h], sems.at[4 + h])
-
-    for h in range(MB):
-        leave(h).start()
+    chunks = plan[2, 0] // BUNCH
+    ready = lax.fori_loop(0, (chunks + CHUNKS - 1) // CHUNKS, several, 0)
+    lax.fori_loop(ready, MB, release, 0)
     for copy in onward:
         copy.wait()
     for h in range(MB):
@@ -600,11 +606,12 @@
             like((8, spaces), i32),
         ),
         in_specs=[pl.BlockSpec(memory_space=pltpu.HBM)] * 9,
-        out_specs=(anywhere,) * 4 + (VMEM,),
+        out_specs=(anywhere,) * 5,
         scratch_shapes=[
             pltpu.VMEM(each.shape, each.dtype)
             for each in inputs + (positions, positions)
         ]
+        + [pltpu.VMEM((8, spaces), i32)]
         + [
             pltpu.VMEM((n * spot_rows, BLK), i32),
             pltpu.VMEM((n * spot_rows, BLK), i32),
@@ -640,16 +647,17 @@
             like(positions.shape, f32),
             like((MB, S * LEV, MBC), f32),
         ),
-        in_specs=[SMEM] + [anywhere] * 4,
+        in_specs=[anywhere] * 5,
         out_specs=(anywhere,) * 3,
         scratch_shapes=[
+            pltpu.SMEM(plan.shape, i32),
             pltpu.VMEM(heights.shape, i32),
             pltpu.VMEM(shares.shape, i32),
             pltpu.VMEM((MB, S * LEV, MBC), f32),
             pltpu.VMEM(positions.shape, f32),
             pltpu.VMEM(positions.shape, f32),
             pltpu.VMEM((2 * MBC, BLK), i32),
-            dma((6 + MB,)),
+            dma((7 + MB,)),
         ],
         name="deposit",
     )(plan, heights, shares, moved, turbulence)

time: 56.1 us -> 54.1 us (0.964)
  Pallas kernels: 54.8 us -> 52.6 us
    pallas_call x1, Pallas kernels: 11.8 us -> 10.2 us  [body(): pl.pallas_call(functools.partial(deposit_kernel, (room, mass_rows, z_rows...]
    pallas_call x1, Pallas kernels: 43 us -> 42.4 us  [body(): pl.pallas_call(functools.partial(advect_kernel, (n_lat, n_lon, blocks, ro...]
where the time goes in v2:
time: 54.1 us; the launch traced here: 53.2 us
  Pallas kernels  52.6 us (97%)
  between operations  0.64 us (1%)
    pallas_call x1, Pallas kernels, body(): pl.pallas_call(functools.partial(advect_kernel, (n_lat, n_lon, blocks, ro...  42.4 us
    pallas_call x1, Pallas kernels, body(): pl.pallas_call(functools.partial(deposit_kernel, (room, mass_rows, z_rows...  10.2 us

profile of v2, /device:TPU:28, one launch (start us, length us, event | category | flops | bytes accessed | tf_op | source)
XLA Modules:
  0.0 53.2 jit_solution(11137888334249820938)
XLA Ops:
  0.6 42.4 %advect.1 = (f32[3,128,128]{2,1,0:T(8,128)}, f32[3,128,128]{2,1,0:T(8,128)}, s32[256,128]{1,0:T(8,128)}, s32[1280,128]{1,0:T(8,128)}, s32[8,384]{1,0:T(8,128)}) custom-call(s32[1,128]{1,0:T(1,128)} %bitcast.19, s32[1,128]{1,0:T(1,128)} %bitcast.20, s32[2,32]{1,0:T(2,128)} %bitcast.18, f32[3,128,128]{2,1,0:T(8,128)} %bitcast.15, f32[3,128,128]{2,1,0:T(8,128)} %bitcast.16, ...), custom_call_target="tpu_custom_call" | custom-call | tf_op jit(solution)/shard_map/advect/pallas_call | solution.py:596
  43.0 10.2 %deposit.1 = (f32[3,128,128]{2,1,0:T(8,128)}, f32[3,128,128]{2,1,0:T(8,128)}, f32[16,320,128]{2,1,0:T(8,128)}) custom-call(s32[8,384]{1,0:T(8,128)} %get-tuple-element.11.plan_in, s32[256,128]{1,0:T(8,128)} %get-tuple-element.12.heights_in, s32[1280,128]{1,0:T(8,128)} %get-tuple-element.13.shares_in, f32[3,128,128]{2,1,0:T(8,128)} %get-tuple-element.14.moved_in, ...), custom_call_target="tpu_custom_call" | custom-call | tf_op jit(solution)/shard_map/deposit/pallas_call | solution.py:643

commit v3 on v2

--- a/solution.py
+++ b/solution.py
@@ -330,7 +330,6 @@
     placing = pltpu.make_async_copy(places, place, local.at[1])
     placing.start()
 
-    mass_mail.post(lats[0])
     mass_mail.post(lats[1])
     for copy in fetches[6:]:
         copy.wait()
@@ -456,6 +455,7 @@
     for copy in leaving:
         copy.start()
     mass_mail.post(lats[2])
+    mass_mail.post(lats[0])
     for copy in leaving:
         copy.wait()
     z_mail.collect()

time: 54.1 us -> 53.6 us (level)
  the two profiles are of different devices: /device:TPU:28 before, /device:TPU:0 now
where the time goes in v3:
time: 53.6 us; the launch traced here: 54.2 us
  Pallas kernels  53.6 us (100%)
  between operations  0.64 us (1%)
    pallas_call x1, Pallas kernels, body(): pl.pallas_call(functools.partial(advect_kernel, (n_lat, n_lon, blocks, ro...  43.4 us
    pallas_call x1, Pallas kernels, body(): pl.pallas_call(functools.partial(deposit_kernel, (room, mass_rows, z_rows...  10.2 us

profile of v3, /device:TPU:0, one launch (start us, length us, event | category | flops | bytes accessed | tf_op | source)
XLA Modules:
  0.0 54.2 jit_solution(4810715430395819089)
XLA Ops:
  0.6 43.4 %advect.1 = (f32[3,128,128]{2,1,0:T(8,128)}, f32[3,128,128]{2,1,0:T(8,128)}, s32[256,128]{1,0:T(8,128)}, s32[1280,128]{1,0:T(8,128)}, s32[8,384]{1,0:T(8,128)}) custom-call(s32[1,128]{1,0:T(1,128)} %bitcast.19, s32[1,128]{1,0:T(1,128)} %bitcast.20, s32[2,32]{1,0:T(2,128)} %bitcast.18, f32[3,128,128]{2,1,0:T(8,128)} %bitcast.15, f32[3,128,128]{2,1,0:T(8,128)} %bitcast.16, ...), custom_call_target="tpu_custom_call" | custom-call | tf_op jit(solution)/shard_map/advect/pallas_call | solution.py:596
  44.0 10.2 %deposit.1 = (f32[3,128,128]{2,1,0:T(8,128)}, f32[3,128,128]{2,1,0:T(8,128)}, f32[16,320,128]{2,1,0:T(8,128)}) custom-call(s32[8,384]{1,0:T(8,128)} %get-tuple-element.11.plan_in, s32[256,128]{1,0:T(8,128)} %get-tuple-element.12.heights_in, s32[1280,128]{1,0:T(8,128)} %get-tuple-element.13.shares_in, f32[3,128,128]{2,1,0:T(8,128)} %get-tuple-element.14.moved_in, ...), custom_call_target="tpu_custom_call" | custom-call | tf_op jit(solution)/shard_map/deposit/pallas_call | solution.py:643
